TPU v7x, 32 devices: a whole 2x2x4 slice. The times are simulated.
32 devices in a mesh: va: 8 (over z, y), vb: 4 (over x, core).
Axes of the slice: x: 2, y: 2, z: 4, core: 2. Of those that a mesh axis runs over, the one named last changes fastest.
Arguments:
- amplitudes: bfloat16 [2, 2, 2048, 2048], P(None, None, 'va', 'vb'), may hold values from -6 to 6
- integrals: bfloat16 [4, 2048, 2048], P(None, 'va', 'vb'), may hold values from -0.125 to 0.125
- occ_energy: float32 [2], replicated, may hold values from -2 to -0.5
- vir_energy: float32 [2048], replicated, may hold values from 0.2 to 3
- screen: int32 [8, 8], replicated, may hold values from -1 to 15, as said below
- lengths: int32 [8], replicated, may hold values from 2 to 8, as said below
Outputs:
- update: float32 [2, 2, 2048, 2048], P(None, None, 'va', 'vb')
Inputs may be any that keep to these rules, and one draw needn't show every extreme that they name: `screen`: row r holds lengths[r] distinct tile numbers below 16 in its first slots and -1 in the others. `lengths`: exactly one grid row lists 8 tiles; every other row lists at most 4.
All inputs are finite; a program needn't handle non-finite values.
Results may differ from a plain program's by a relative error of at most 0.0031.
Values may be sent and summed in bfloat16 or wider, within the bound.
A program may use at most 64 MiB of HBM per device.

v0:
```python
import jax
import jax.numpy as jnp
from jax import lax
from jax.sharding import PartitionSpec as P

TILE = 128


def from_root(value, axis, source):
    kept = jnp.where(lax.axis_index(axis) == source, value, 0).astype(value.dtype)
    return lax.psum(kept, axis)


def tile_terms(spin_tile, k_rows):
    occ_count = spin_tile.shape[0]
    blocks = k_rows.reshape(occ_count, occ_count, k_rows.shape[1], k_rows.shape[2])
    return jnp.einsum("ikac,kjcb->ijab", spin_tile, blocks, preferred_element_type=jnp.float32)


def local(amplitudes, integrals, occ_energy, vir_energy, screen, lengths):
    count_va = lax.axis_size("va")
    count_vb = lax.axis_size("vb")
    occ_a, occ_b, row_len, col_len = amplitudes.shape
    ratio = count_va // count_vb
    slab = row_len // count_vb
    section_one = lax.all_to_all(amplitudes, "vb", split_axis=2, concat_axis=3, tiled=True)
    section_two = lax.all_to_all(
        lax.all_to_all(section_one, "va", split_axis=3, concat_axis=2, tiled=True),
        "vb",
        split_axis=2,
        concat_axis=2,
        tiled=True,
    )
    regroup = section_two.reshape(occ_a, occ_b, count_vb, ratio, slab, row_len)
    regroup = jnp.transpose(regroup, (0, 1, 3, 2, 4, 5)).reshape(occ_a, occ_b, col_len, row_len)
    mirror = jnp.swapaxes(regroup, 2, 3)
    spin_amp = (2.0 * amplitudes.astype(jnp.float32) - mirror.astype(jnp.float32)).astype(
        jnp.bfloat16
    )
    whole_k = lax.all_gather(integrals, "va", axis=1, tiled=True)
    zeros_r = jnp.zeros((occ_a, occ_b, row_len, col_len), jnp.float32)
    my_row = lax.axis_index("va")
    tile_ids = screen[my_row]
    row_count = lengths[my_row]
    slots = screen.shape[1]
    per_shard = col_len // TILE

    def own_piece(source, tile_id):
        offset = tile_id % per_shard * TILE
        return (lax.dynamic_slice_in_dim(source, offset, TILE, 3), tile_id // per_shard)

    def integral_rows(tile_id):
        return lax.dynamic_slice_in_dim(whole_k, tile_id * TILE, TILE, 1)

    def padded_slot(slot_no, accum_r):
        tile_id = jnp.maximum(tile_ids[slot_no], 0)
        own_tile, owner_id = own_piece(spin_amp, tile_id)
        arrived = from_root(own_tile, "vb", owner_id)
        is_live = (slot_no < row_count).astype(jnp.float32)
        return accum_r + is_live * tile_terms(arrived, integral_rows(tile_id))

    accum = lax.fori_loop(0, slots, padded_slot, zeros_r)
    vir_rows = lax.dynamic_slice_in_dim(vir_energy, my_row * row_len, row_len)
    vir_cols = lax.dynamic_slice_in_dim(vir_energy, lax.axis_index("vb") * col_len, col_len)
    denominator = (
        occ_energy[:, None, None, None]
        + occ_energy[None, :, None, None]
        - vir_rows[None, None, :, None]
        - vir_cols[None, None, None, :]
    )
    return accum / denominator


def solution(mesh):
    return jax.shard_map(
        local,
        mesh=mesh,
        in_specs=(P(None, None, "va", "vb"), P(None, "va", "vb"), P(), P(), P(), P()),
        out_specs=P(None, None, "va", "vb"),
        check_vma=False,
    )
```

profile of v0, /device:TPU:0, one launch (start us, length us, event | category | flops | bytes accessed | tf_op | source)
XLA Modules:
  0.0 465.9 jit_solution(7897974727014326914)
XLA Ops:
  7.3 2.3 copy.27
  9.6 18.5 %all_to_all.41 = bf16[2,2,256,512]{3,1,0,2:T(2,128)(2,1)S(1)} all-to-all(bf16[2,2,256,512]{3,1,0,2:T(2,128)(2,1)S(1)} %copy.27), channel_id=1, replica_groups=mesh['va'=8,'vb'=4] {'vb'}, dimensions={2} | all-to-all | bytes 2097152 | tf_op jit(solution)/shard_map/all_to_all | solution.py:26
  28.9 3.2 copy.39
  32.1 1.7 reshape.73
  33.8 47.6 %all_to_all.42 = bf16[8,2,32768]{2,1,0:T(2,128)(2,1)} all-to-all(bf16[8,2,32768]{2,1,0:T(2,128)(2,1)S(1)} %reshape.73), channel_id=1, replica_groups=mesh['va'=8,'vb'=4] {'va'}, dimensions={0} | all-to-all | bytes 2097152 | tf_op jit(solution)/shard_map/all_to_all | solution.py:28
  81.4 3.2 reshape.74
  84.6 2.8 copy.41
  87.3 2.0 copy.32
  89.4 3.6 all-to-all-start.2
  93.1 1.4 copy.26
  96.8 10.7 %all-to-all-done.2 = bf16[2,2,512,256]{3,1,0,2:T(2,128)(2,1)S(1)} async-done(((bf16[2,2,512,256]{3,1,0,2:T(2,128)(2,1)}), bf16[2,2,512,256]{3,1,0,2:T(2,128)(2,1)S(1)}, u32[]{:S(2)}, u32[]{:S(2)}) %all-to-all-start.2) | async-done | bytes 1048608 | tf_op jit(solution)/shard_map/all_to_all | solution.py:27
  109.1 1.3 fusion.2
  110.4 45.8 %all-gather.2.cloned.1.call-done = bf16[4,2048,512]{2,1,0:T(8,128)(2,1)} async-done(((bf16[4,256,512]{2,1,0:T(8,128)(2,1)}), bf16[4,2048,512]{2,1,0:T(8,128)(2,1)}) %all-gather.2.cloned.1.call-update) | async-done | bytes 8388624 | tf_op jit(solution)/shard_map/all_gather | solution.py:40
  156.2 298.1 %while.16 = (s32[]{:T(128)}, f32[2,2,256,512]{2,3,0,1:T(8,128)S(1)}, s32[]{:T(128)}, s32[8]{0:T(128)S(1)}, bf16[4,2048,512]{2,1,0:T(8,128)(2,1)}, /*index=5*/bf1...) while((s32[]{:T(128)}, ...), condition=%wide.region_2.3_spmd.clone, body=%wide.region_0.2_spmd.clone.sunk | while | flops 270270496 | bytes 9175550 | solution.py:62
  161.1 28.8 %all-reduce.2.cloned.1.call-done = bf16[2,2,256,128]{3,2,1,0:T(8,128)(2,1)} async-done(((bf16[2,2,256,128]{3,2,1,0:T(8,128)(2,1)}), bf16[2,2,256,128]{3,2,1,0:T(8,128)(2,1)}) %all-reduce.2.cloned.1.call-update) | async-done | bytes 262160 | tf_op jit(solution)/shard_map/while/body/eval_jaxpr/psum | solution.py:11
  189.9 1.9 bitcast_add_fusion.2
  196.8 30.6 %all-reduce.2.cloned.1.call-done = bf16[2,2,256,128]{3,2,1,0:T(8,128)(2,1)} async-done(((bf16[2,2,256,128]{3,2,1,0:T(8,128)(2,1)}), bf16[2,2,256,128]{3,2,1,0:T(8,128)(2,1)}) %all-reduce.2.cloned.1.call-update) | async-done | bytes 262160 | tf_op jit(solution)/shard_map/while/body/eval_jaxpr/psum | solution.py:11
  227.4 1.9 bitcast_add_fusion.2
  234.3 30.6 %all-reduce.2.cloned.1.call-done = bf16[2,2,256,128]{3,2,1,0:T(8,128)(2,1)} async-done(((bf16[2,2,256,128]{3,2,1,0:T(8,128)(2,1)}), bf16[2,2,256,128]{3,2,1,0:T(8,128)(2,1)}) %all-reduce.2.cloned.1.call-update) | async-done | bytes 262160 | tf_op jit(solution)/shard_map/while/body/eval_jaxpr/psum | solution.py:11
  264.9 1.9 bitcast_add_fusion.2
  271.8 30.6 %all-reduce.2.cloned.1.call-done = bf16[2,2,256,128]{3,2,1,0:T(8,128)(2,1)} async-done(((bf16[2,2,256,128]{3,2,1,0:T(8,128)(2,1)}), bf16[2,2,256,128]{3,2,1,0:T(8,128)(2,1)}) %all-reduce.2.cloned.1.call-update) | async-done | bytes 262160 | tf_op jit(solution)/shard_map/while/body/eval_jaxpr/psum | solution.py:11
  302.4 1.9 bitcast_add_fusion.2
  309.3 30.6 %all-reduce.2.cloned.1.call-done = bf16[2,2,256,128]{3,2,1,0:T(8,128)(2,1)} async-done(((bf16[2,2,256,128]{3,2,1,0:T(8,128)(2,1)}), bf16[2,2,256,128]{3,2,1,0:T(8,128)(2,1)}) %all-reduce.2.cloned.1.call-update) | async-done | bytes 262160 | tf_op jit(solution)/shard_map/while/body/eval_jaxpr/psum | solution.py:11
  339.9 1.9 bitcast_add_fusion.2
  346.8 30.6 %all-reduce.2.cloned.1.call-done = bf16[2,2,256,128]{3,2,1,0:T(8,128)(2,1)} async-done(((bf16[2,2,256,128]{3,2,1,0:T(8,128)(2,1)}), bf16[2,2,256,128]{3,2,1,0:T(8,128)(2,1)}) %all-reduce.2.cloned.1.call-update) | async-done | bytes 262160 | tf_op jit(solution)/shard_map/while/body/eval_jaxpr/psum | solution.py:11
  377.4 1.9 bitcast_add_fusion.2
  384.3 30.6 %all-reduce.2.cloned.1.call-done = bf16[2,2,256,128]{3,2,1,0:T(8,128)(2,1)} async-done(((bf16[2,2,256,128]{3,2,1,0:T(8,128)(2,1)}), bf16[2,2,256,128]{3,2,1,0:T(8,128)(2,1)}) %all-reduce.2.cloned.1.call-update) | async-done | bytes 262160 | tf_op jit(solution)/shard_map/while/body/eval_jaxpr/psum | solution.py:11
  414.9 1.9 bitcast_add_fusion.2
  421.8 30.6 %all-reduce.2.cloned.1.call-done = bf16[2,2,256,128]{3,2,1,0:T(8,128)(2,1)} async-done(((bf16[2,2,256,128]{3,2,1,0:T(8,128)(2,1)}), bf16[2,2,256,128]{3,2,1,0:T(8,128)(2,1)}) %all-reduce.2.cloned.1.call-update) | async-done | bytes 262160 | tf_op jit(solution)/shard_map/while/body/eval_jaxpr/psum | solution.py:11
  452.4 1.9 bitcast_add_fusion.2
  454.3 1.8 copy.36
  456.1 3.3 subtract_divide_fusion
  (79 shorter events, 34.4 us)
Async XLA Ops:
  6.5 90.1 %copy-start = (s32[8,8]{1,0:T(8,128)S(1)}, s32[8,8]{1,0:T(8,128)}, u32[]{:S(2)}) copy-start(s32[8,8]{1,0:T(8,128)} %param.12) | copy-start | bytes 772
  6.5 149.7 %all-gather.2.cloned.1.call-start = ((), (), s32[]{:S(2)}) async-start(), calls=%async_computation.3 | async-start | bytes 9437184 | tf_op jit(solution)/shard_map/all_gather | solution.py:40
  87.3 5.7 %copy-start.1 = (bf16[2,2,256,512]{3,2,1,0:T(8,128)(2,1)S(1)}, bf16[2,2,256,512]{3,2,1,0:T(8,128)(2,1)}, u32[]{:S(2)}) copy-start(bf16[2,2,256,512]{3,2,1,0:T(8,128)(2,1)} %param.8) | copy-start | bytes 3145732
  89.4 6.6 %copy-start.4 = (s32[8]{0:T(128)S(1)}, s32[8]{0:T(128)}, u32[]{:S(2)}) copy-start(s32[8]{0:T(128)} %param.13) | copy-start | bytes 100
  89.4 7.2 %copy-start.3 = (f32[2]{0:T(128)S(1)}, f32[2]{0:T(128)}, u32[]{:S(2)}) copy-start(f32[2]{0:T(128)} %param.10) | copy-start | bytes 28
  89.4 18.1 %all-to-all-start.2 = ((bf16[2,2,512,256]{3,1,0,2:T(2,128)(2,1)}), bf16[2,2,512,256]{3,1,0,2:T(2,128)(2,1)S(1)}, u32[]{:S(2)}, u32[]{:S(2)}) async-start(bf16[2,2,512,256]{3,1,0,2:T(2,128)(2,1)} %copy.32), calls=%async_computation.2 | async-start | bytes 2097152 | tf_op jit(solution)/shard_map/all_to_all | solution.py:27
  107.8 1.2 copy-start.2
  156.2 33.7 %all-reduce.2.cloned.1.call-start = ((), (), s32[]{:S(2)}) async-start(), calls=%async_computation.4 | async-start | bytes 524288 | tf_op jit(solution)/shard_map/while/body/eval_jaxpr/psum | solution.py:11
  191.8 35.6 %all-reduce.2.cloned.1.call-start = ((), (), s32[]{:S(2)}) async-start(), calls=%async_computation.4 | async-start | bytes 524288 | tf_op jit(solution)/shard_map/while/body/eval_jaxpr/psum | solution.py:11
  229.3 35.6 %all-reduce.2.cloned.1.call-start = ((), (), s32[]{:S(2)}) async-start(), calls=%async_computation.4 | async-start | bytes 524288 | tf_op jit(solution)/shard_map/while/body/eval_jaxpr/psum | solution.py:11
  266.8 35.6 %all-reduce.2.cloned.1.call-start = ((), (), s32[]{:S(2)}) async-start(), calls=%async_computation.4 | async-start | bytes 524288 | tf_op jit(solution)/shard_map/while/body/eval_jaxpr/psum | solution.py:11
  304.3 35.6 %all-reduce.2.cloned.1.call-start = ((), (), s32[]{:S(2)}) async-start(), calls=%async_computation.4 | async-start | bytes 524288 | tf_op jit(solution)/shard_map/while/body/eval_jaxpr/psum | solution.py:11
  341.8 35.6 %all-reduce.2.cloned.1.call-start = ((), (), s32[]{:S(2)}) async-start(), calls=%async_computation.4 | async-start | bytes 524288 | tf_op jit(solution)/shard_map/while/body/eval_jaxpr/psum | solution.py:11
  379.3 35.6 %all-reduce.2.cloned.1.call-start = ((), (), s32[]{:S(2)}) async-start(), calls=%async_computation.4 | async-start | bytes 524288 | tf_op jit(solution)/shard_map/while/body/eval_jaxpr/psum | solution.py:11
  416.8 35.6 %all-reduce.2.cloned.1.call-start = ((), (), s32[]{:S(2)}) async-start(), calls=%async_computation.4 | async-start | bytes 524288 | tf_op jit(solution)/shard_map/while/body/eval_jaxpr/psum | solution.py:11
Sparse Core Ops, SparseCore 0:
  9.5 146.6 all-gather.1
  159.4 30.4 all-reduce.1
  195.1 32.2 all-reduce.1
  232.6 32.2 all-reduce.1
  270.1 32.2 all-reduce.1
  307.6 32.2 all-reduce.1
  345.1 32.2 all-reduce.1
  382.6 32.2 all-reduce.1
  420.1 32.2 all-reduce.1
where the time goes:
time: 467 us; the launch traced here: 466 us
  waiting for transfers between devices  301 us (64%)
  blocking collectives  66 us (14%)
  local copies, waits for them, and re-layouts  45.3 us (10%)
  matrix products  15 us (3%)
  between operations  13.2 us (3%)
  other arithmetic  11 us (2%)
  loops' own time  10.8 us (2%)
    psum x8, waiting for transfers between devices, from_root(): return lax.psum(kept, axis)  243 us
    all_to_all x1, blocking collectives, local(): lax.all_to_all(section_one, 'va', split_axis=3, concat_axis=2, tiled=True)  47.6 us
    all_gather x1, waiting for transfers between devices, local(): whole_k = lax.all_gather(integrals, 'va', axis=1, tiled=True)  45.8 us
    all_to_all x1, blocking collectives, local(): lax.all_to_all(amplitudes, 'vb', split_axis=2, concat_axis=3, tiled=True)  18.5 us
    dot_general x8, matrix products, tile_terms(): jnp.einsum('ikac,kjcb->ijab', spin_tile, blocks, preferred_element_type=j...  15 us
    another operation x1, loops' own time, local(): accum = lax.fori_loop(0, slots, padded_slot, zeros_r)  10.8 us
    all_to_all x1, waiting for transfers between devices, local(): lax.all_to_all(lax.all_to_all(section_one, 'va', split_axis=3, concat_axi...  10.7 us
    unnamed x14, local copies, waits for them, and re-layouts  9.57 us
  transfers between devices with their start and end apart: 10, of which 10 were waited for; matrix products, arithmetic and copies ran while one was open for 7% of the time, Pallas kernels for 0%

commit v1 on v0

v1 whole, which is shorter than its diff:
```python
import functools

import jax
import jax.numpy as jnp
from jax import lax
from jax.experimental import pallas as pl
from jax.experimental.pallas import tpu as pltpu
from jax.sharding import PartitionSpec as P

TILE = 128
PAIR = 2
MESH = pl.DeviceIdType.MESH


def gather_kernel(
    count_va, count_vb, amp_ref, turned_ref, int_ref, whole_k, spin_all,
    landed, spin, z_send, z_recv, y_send, y_recv, m_send, m_recv, s_send, s_recv, own_sem,
):
    va = lax.axis_index("va")
    vb = lax.axis_index("vb")
    ratio = count_va // count_vb
    lines = count_va // PAIR
    outers = count_vb // PAIR
    line, side = va // PAIR, va % PAIR
    outer, core = vb // PAIR, vb % PAIR
    chunks, rows, _ = int_ref.shape
    row_len = amp_ref.shape[2]

    def k_slot(owner, chunk):
        return whole_k.at[chunk, pl.ds(pl.multiple_of(owner * rows, rows), rows)]

    def remote(src, dst, send, recv, target):
        return pltpu.make_async_remote_copy(
            src_ref=src, dst_ref=dst, send_sem=send, recv_sem=recv, device_id=target, device_id_type=MESH
        )

    def mirror_copy(part):
        return remote(
            turned_ref.at[part], landed.at[va % ratio], m_send.at[part], m_recv.at[va % ratio],
            {"va": vb * ratio + part, "vb": va // ratio},
        )

    def mirror_arrival(part):
        return remote(
            turned_ref.at[part], landed.at[part], m_send.at[part], m_recv.at[part],
            {"va": vb * ratio + part, "vb": va // ratio},
        )

    def mirror_own(part):
        return pltpu.make_async_copy(turned_ref.at[part], landed.at[part], m_recv.at[part])

    for part in range(ratio):
        is_own = va == vb * ratio + part

        @pl.when(is_own)
        def _():
            mirror_own(part).start()

        @pl.when(jnp.logical_not(is_own))
        def _():
            mirror_copy(part).start()

    def source(direction, step):
        return line - step if direction == 0 else line + step

    def block_at(direction, step, chunk):
        if step == 0:
            return int_ref.at[chunk]
        return k_slot(source(direction, step) * PAIR + side, chunk)

    def line_send(direction, step, chunk):
        to = line + 1 if direction == 0 else line - 1
        return remote(
            block_at(direction, step, chunk),
            k_slot(source(direction, step) * PAIR + side, chunk),
            z_send.at[direction, step, chunk],
            z_recv.at[direction, step, chunk],
            {"va": to * PAIR + side},
        )

    def line_arrival(direction, step, chunk):
        here = k_slot(source(direction, step) * PAIR + side, chunk)
        return remote(
            here, here, z_send.at[direction, step - 1, chunk], z_recv.at[direction, step - 1, chunk],
            {"va": va},
        )

    def may_send(direction, step):
        if direction == 0:
            return jnp.logical_and(line - step >= 0, line + 1 < lines)
        return jnp.logical_and(line + step < lines, line - 1 >= 0)

    def has_arrival(direction, step):
        return line - step >= 0 if direction == 0 else line + step < lines

    def side_send(direction, step, chunk):
        return remote(
            block_at(direction, step, chunk),
            k_slot(source(direction, step) * PAIR + side, chunk),
            y_send.at[direction, step, chunk],
            y_recv.at[direction, step, chunk],
            {"va": line * PAIR + 1 - side},
        )

    def side_arrival(direction, step, chunk):
        here = k_slot(source(direction, step) * PAIR + 1 - side, chunk)
        return remote(
            here, here, y_send.at[direction, step, chunk], y_recv.at[direction, step, chunk], {"va": va}
        )

    def own_copy(chunk):
        return pltpu.make_async_copy(int_ref.at[chunk], k_slot(va, chunk), own_sem.at[chunk])

    for chunk in range(chunks):
        for direction in range(2):

            @pl.when(may_send(direction, 0))
            def _():
                line_send(direction, 0, chunk).start()

        side_send(0, 0, chunk).start()
    for chunk in range(chunks):
        own_copy(chunk).start()

    def line_step(step):
        for chunk in range(chunks):
            for direction in range(2):

                @pl.when(has_arrival(direction, step))
                def _():
                    line_arrival(direction, step, chunk).wait_recv()

                    @pl.when(may_send(direction, step))
                    def _():
                        line_send(direction, step, chunk).start()

                    side_send(direction, step, chunk).start()

    def spin_send(shift):
        to = lax.rem(outer + shift, outers)
        return remote(
            spin, spin_all.at[vb], s_send.at[0, shift], s_recv.at[0, shift], {"vb": to * PAIR + core}
        )

    def spin_arrival(shift):
        here = spin_all.at[lax.rem(outer + outers - shift, outers) * PAIR + core]
        return remote(here, here, s_send.at[0, shift], s_recv.at[0, shift], {"vb": vb})

    def spin_relay(shift):
        held = spin_all.at[lax.rem(outer + outers - shift, outers) * PAIR + core]
        src = spin if shift == 0 else held
        return remote(
            src, held, s_send.at[1, shift], s_recv.at[1, shift], {"vb": outer * PAIR + 1 - core}
        )

    def relay_arrival(shift):
        here = spin_all.at[lax.rem(outer + outers - shift, outers) * PAIR + 1 - core]
        return remote(here, here, s_send.at[1, shift], s_recv.at[1, shift], {"vb": vb})

    def spin_own():
        return pltpu.make_async_copy(spin, spin_all.at[vb], own_sem.at[chunks])

    def spin_step():
        for part in range(ratio):
            is_own = va == vb * ratio + part

            @pl.when(is_own)
            def _():
                mirror_own(part).wait()

            @pl.when(jnp.logical_not(is_own))
            def _():
                mirror_arrival(part).wait_recv()

            cols = slice(part * row_len, (part + 1) * row_len)
            spin[:, :, :, cols] = (
                2.0 * amp_ref[:, :, :, cols].astype(jnp.float32) - landed[part].astype(jnp.float32)
            ).astype(spin.dtype)
        for shift in range(1, outers):
            spin_send(shift).start()
        spin_relay(0).start()
        spin_own().start()

    for step in range(1, lines):
        line_step(step)
        if step == 1:
            spin_step()
    if lines == 1:
        spin_step()
    for shift in range(1, outers):
        spin_arrival(shift).wait_recv()
        spin_relay(shift).start()

    for chunk in range(chunks):
        own_copy(chunk).wait()
        side_arrival(0, 0, chunk).wait_recv()
        side_send(0, 0, chunk).wait_send()
        for direction in range(2):

            @pl.when(may_send(direction, 0))
            def _():
                line_send(direction, 0, chunk).wait_send()

    for step in range(1, lines):
        for chunk in range(chunks):
            for direction in range(2):

                @pl.when(may_send(direction, step))
                def _():
                    line_send(direction, step, chunk).wait_send()

                @pl.when(has_arrival(direction, step))
                def _():
                    side_arrival(direction, step, chunk).wait_recv()
                    side_send(direction, step, chunk).wait_send()

    for part in range(ratio):

        @pl.when(jnp.logical_not(va == vb * ratio + part))
        def _():
            mirror_copy(part).wait_send()

    spin_own().wait()
    for shift in range(outers):
        relay_arrival(shift).wait_recv()
        spin_relay(shift).wait_send()
    for shift in range(1, outers):
        spin_send(shift).wait_send()


def gather_all(amplitudes, turned, integrals, count_va, count_vb):
    occ_a, occ_b, row_len, col_len = amplitudes.shape
    chunks, rows, cols = integrals.shape
    ratio = count_va // count_vb
    lines = count_va // PAIR
    outers = count_vb // PAIR
    dma = pltpu.SemaphoreType.DMA
    return pl.pallas_call(
        functools.partial(gather_kernel, count_va, count_vb),
        out_shape=(
            jax.ShapeDtypeStruct((chunks, count_va * rows, cols), integrals.dtype),
            jax.ShapeDtypeStruct((count_vb, occ_a, occ_b, row_len, col_len), amplitudes.dtype),
        ),
        in_specs=[pl.BlockSpec(memory_space=pltpu.VMEM)] * 3,
        out_specs=(pl.BlockSpec(memory_space=pl.ANY),) * 2,
        scratch_shapes=[
            pltpu.VMEM(turned.shape, turned.dtype),
            pltpu.VMEM(amplitudes.shape, amplitudes.dtype),
            dma((2, lines, chunks)),
            dma((2, lines, chunks)),
            dma((2, lines, chunks)),
            dma((2, lines, chunks)),
            dma((ratio,)),
            dma((ratio,)),
            dma((2, outers)),
            dma((2, outers)),
            dma((chunks + 1,)),
        ],
        compiler_params=pltpu.CompilerParams(has_side_effects=True),
    )(amplitudes, turned, integrals)


def cycle_kernel(per_shard, ids, count, occ, spin_ref, k_ref, rows_ref, cols_ref, out_ref):
    slot = pl.program_id(0)
    occ_count = spin_ref.shape[1]

    @pl.when(slot == 0)
    def _():
        out_ref[...] = jnp.zeros_like(out_ref)

    @pl.when(slot < count[0])
    def _():
        for j in range(occ_count):
            right = jnp.concatenate([k_ref[k * occ_count + j] for k in range(occ_count)], axis=0)
            for i in range(occ_count):
                left = jnp.concatenate([spin_ref[0, i, k] for k in range(occ_count)], axis=1)
                out_ref[i, j] += jnp.dot(left, right, preferred_element_type=jnp.float32)

    @pl.when(slot == pl.num_programs(0) - 1)
    def _():
        for i in range(occ_count):
            for j in range(occ_count):
                bottom = (occ[i] + occ[j] - rows_ref[...]) - cols_ref[...]
                out_ref[i, j] = out_ref[i, j] / bottom


def local(amplitudes, integrals, occ_energy, vir_energy, screen, lengths):
    count_va = lax.axis_size("va")
    count_vb = lax.axis_size("vb")
    occ_a, occ_b, row_len, col_len = amplitudes.shape
    ratio = count_va // count_vb
    cols = integrals.shape[2]
    turned = jnp.transpose(
        amplitudes.reshape(occ_a, occ_b, row_len, ratio, row_len), (3, 0, 1, 4, 2)
    )
    whole_k, spin_all = gather_all(amplitudes, turned, integrals, count_va, count_vb)
    my_row = lax.axis_index("va")
    slots = screen.shape[1]
    per_shard = col_len // TILE
    row_count = lax.dynamic_slice_in_dim(lengths, my_row, 1)
    ids = lax.dynamic_index_in_dim(screen, my_row, 0, keepdims=False)
    ids = jnp.maximum(ids[jnp.minimum(jnp.arange(slots), row_count[0] - 1)], 0)
    vir_rows = lax.dynamic_slice_in_dim(vir_energy, my_row * row_len, row_len)[:, None]
    vir_cols = lax.dynamic_slice_in_dim(vir_energy, lax.axis_index("vb") * cols, cols)[None, :]
    return pl.pallas_call(
        functools.partial(cycle_kernel, per_shard),
        out_shape=jax.ShapeDtypeStruct((occ_a, occ_b, row_len, cols), jnp.float32),
        grid_spec=pltpu.PrefetchScalarGridSpec(
            num_scalar_prefetch=3,
            grid=(slots,),
            in_specs=[
                pl.BlockSpec(
                    (1, occ_a, occ_b, row_len, TILE),
                    lambda m, ids, count, occ: (ids[m] // per_shard, 0, 0, 0, ids[m] % per_shard),
                ),
                pl.BlockSpec((integrals.shape[0], TILE, cols), lambda m, ids, count, occ: (0, ids[m], 0)),
                pl.BlockSpec((row_len, 1), lambda m, ids, count, occ: (0, 0)),
                pl.BlockSpec((1, cols), lambda m, ids, count, occ: (0, 0)),
            ],
            out_specs=pl.BlockSpec(
                (occ_a, occ_b, row_len, cols), lambda m, ids, count, occ: (0, 0, 0, 0)
            ),
        ),
    )(ids, row_count, occ_energy, spin_all, whole_k, vir_rows, vir_cols)


def solution(mesh):
    return jax.shard_map(
        local,
        mesh=mesh,
        in_specs=(P(None, None, "va", "vb"), P(None, "va", "vb"), P(), P(), P(), P()),
        out_specs=P(None, None, "va", "vb"),
        check_vma=False,
    )
```

time: 467 us -> 146 us (0.31)
  the two profiles are of different devices: /device:TPU:0 before, /device:TPU:18 now
where the time goes in v1:
time: 146 us; the launch traced here: 145 us
  Pallas kernels  137 us (94%)
  local copies, waits for them, and re-layouts  7.29 us (5%)
    pallas_call x1, Pallas kernels, gather_all(): pl.pallas_call(functools.partial(gather_kernel, count_va, count_vb), out_...  131 us
    pallas_call x1, Pallas kernels, local(): pl.pallas_call(functools.partial(cycle_kernel, per_shard), out_shape=jax....  5.66 us

profile of v1, /device:TPU:18, one launch (start us, length us, event | category | flops | bytes accessed | tf_op | source)
XLA Modules:
  0.0 145.4 jit_solution(15671110907657376934)
XLA Ops:
  0.0 0.0 copy-start
  0.0 1.2 dynamic_slice.14.count
  1.8 0.0 copy-done
  1.8 0.8 dynamic_slice.15
  2.6 1.3 dynamic_slice.16
  3.9 0.6 gather_fusion
  4.6 0.5 broadcast_maximum_fusion.ids
  5.1 0.8 copy.9.rows_ref
  5.9 1.5 %copy.7 = bf16[2,2,256,512]{2,3,1,0:T(8,128)(2,1)S(1)} copy(bf16[2,2,256,512]{3,2,1,0:T(8,128)(2,1)} %amp_ref.1) | data formatting | bytes 2097152 | tf_op args[0]
  7.4 1.0 copy.11
  8.4 131.3 %shard_map.64 = (bf16[4,2048,512]{2,1,0:T(8,128)(2,1)}, bf16[4,2,2,256,512]{4,3,2,1,0:T(8,128)(2,1)}) custom-call(bf16[2,2,256,512]{3,2,1,0:T(8,128)(2,1)} %amp_ref.1, bf16[2,2,2,256,256]{4,3,2,1,0:T(8,128)(2,1)} %bitcast.11, bf16[4,256,512]{2,1,0:T(8,128)(2,1)} %int_ref.1), custom_call_target="tpu_custom_call" | custom-call | tf_op jit(solution)/shard_map/pallas_call | solution.py:238
  139.7 5.7 %shard_map.65 = f32[2,2,256,512]{3,2,1,0:T(8,128)} custom-call(s32[8]{0:T(128)} %broadcast_maximum_fusion.ids, s32[1]{0:T(128)} %dynamic_slice.14.count, f32[2]{0:T(128)} %occ.1, bf16[4,2,2,256,512]{4,3,2,1,0:T(8,128)(2,1)} %get-tuple-element.7.spin_ref, bf16[4,2048,512]{2,1,0:T(8,128)(2,1)} %get-tuple-element.8.k_ref, f32[256,1]{1,0:T(8,128)} %copy.9.rows_ref, ...), custom_call_target="tpu_custom_call" | custom-call | tf_op jit(solution)/shard_map/pallas_call | solution.py:305
  (3 shorter events, 0.0 us)
Async XLA Ops:
  0.0 1.8 %copy-start = (s32[8,8]{1,0:T(8,128)S(1)}, s32[8,8]{1,0:T(8,128)}, u32[]{:S(2)}) copy-start(s32[8,8]{1,0:T(8,128)} %param.10) | copy-start | bytes 772

commit v2 on v1

v2 whole, which is shorter than its diff:
```python
import functools

import jax
import jax.numpy as jnp
from jax import lax
from jax.experimental import pallas as pl
from jax.experimental.pallas import tpu as pltpu
from jax.sharding import PartitionSpec as P

TILE = 128
PAIR = 2
SPLIT = 2
MESH = pl.DeviceIdType.MESH


def gather_kernel(
    count_va, count_vb, amp_ref, turned_ref, int_ref, whole_k, spin_all,
    landed, passing, spin, z_send, z_recv, y_send, y_recv, m_send, m_recv, x_send, x_recv, s_send, s_recv, own_sem,
):
    va = lax.axis_index("va")
    vb = lax.axis_index("vb")
    ratio = count_va // count_vb
    lines = count_va // PAIR
    outers = count_vb // PAIR
    line, side = va // PAIR, va % PAIR
    outer, core = vb // PAIR, vb % PAIR
    blocks, rows, _ = int_ref.shape
    part_rows = rows // SPLIT
    chunks = blocks * SPLIT
    early = chunks - 1
    halves = amp_ref.shape[0]
    row_len = amp_ref.shape[2]

    def k_slot(owner, chunk):
        begin = owner * rows + chunk % SPLIT * part_rows
        return whole_k.at[chunk // SPLIT, pl.ds(pl.multiple_of(begin, part_rows), part_rows)]

    def own_slot(chunk):
        return int_ref.at[chunk // SPLIT, pl.ds(chunk % SPLIT * part_rows, part_rows)]

    def remote(src, dst, send, recv, target):
        return pltpu.make_async_remote_copy(
            src_ref=src, dst_ref=dst, send_sem=send, recv_sem=recv, device_id=target, device_id_type=MESH
        )

    next_vb = lax.rem(outer + 1, outers) * PAIR + core
    last_vb = lax.rem(outer + outers - 1, outers) * PAIR + core

    def by_relay(half):
        return outers > 1 and half % 2 == 1

    def mirror_own(part):
        return pltpu.make_async_copy(turned_ref.at[part], landed.at[part], own_sem.at[part])

    def mirror_straight(part, half):
        return remote(
            turned_ref.at[part, half], landed.at[va % ratio, half],
            m_send.at[0, part, half], m_recv.at[va % ratio, half],
            {"va": vb * ratio + part, "vb": va // ratio},
        )

    def mirror_out(part, half):
        return remote(
            turned_ref.at[part, half], passing.at[part, half],
            x_send.at[part, half], x_recv.at[part, half], {"vb": next_vb},
        )

    def mirror_on(part, half):
        return remote(
            passing.at[part, half], landed.at[va % ratio, half],
            m_send.at[1, part, half], m_recv.at[va % ratio, half],
            {"va": last_vb * ratio + part, "vb": va // ratio},
        )

    def mirror_passing(part, half):
        here = passing.at[part, half]
        return remote(here, here, x_send.at[part, half], x_recv.at[part, half], {"vb": vb})

    def mirror_arrival(part, half):
        here = landed.at[part, half]
        return remote(here, here, m_send.at[0, part, half], m_recv.at[part, half], {"vb": vb})

    def stays(part):
        return va == vb * ratio + part

    def last_stays(part):
        return va == last_vb * ratio + part

    def each_mirror(own, straight, out):
        for part in range(ratio):

            @pl.when(stays(part))
            def _():
                own(part)

            @pl.when(jnp.logical_not(stays(part)))
            def _():
                for half in range(halves):
                    (out if by_relay(half) else straight)(part, half)

    each_mirror(
        lambda part: mirror_own(part).start(),
        lambda part, half: mirror_straight(part, half).start(),
        lambda part, half: mirror_out(part, half).start(),
    )

    def each_passing(act):
        for part in range(ratio):

            @pl.when(jnp.logical_not(last_stays(part)))
            def _():
                for half in range(halves):
                    if by_relay(half):
                        act(part, half)

    def source(direction, step):
        return line - step if direction == 0 else line + step

    def line_slot(direction, step, chunk):
        if chunk == chunks:
            return k_slot(source(direction, step) * PAIR + 1 - side, early)
        return k_slot(source(direction, step) * PAIR + side, chunk)

    def block_at(direction, step, chunk):
        if step == 0 and chunk < chunks:
            return own_slot(chunk)
        return line_slot(direction, step, chunk)

    def line_send(direction, step, chunk):
        to = line + 1 if direction == 0 else line - 1
        return remote(
            block_at(direction, step, chunk),
            line_slot(direction, step, chunk),
            z_send.at[direction, step, chunk],
            z_recv.at[direction, step, chunk],
            {"va": to * PAIR + side},
        )

    def line_arrival(direction, step, chunk):
        here = line_slot(direction, step, chunk)
        return remote(
            here, here, z_send.at[direction, step - 1, chunk], z_recv.at[direction, step - 1, chunk],
            {"va": va},
        )

    def may_send(direction, step):
        if direction == 0:
            return jnp.logical_and(line - step >= 0, line + 1 < lines)
        return jnp.logical_and(line + step < lines, line - 1 >= 0)

    def has_arrival(direction, step):
        return line - step >= 0 if direction == 0 else line + step < lines

    def side_send(direction, step, chunk):
        return remote(
            block_at(direction, step, chunk),
            line_slot(direction, step, chunk),
            y_send.at[direction, step, chunk],
            y_recv.at[direction, step, chunk],
            {"va": line * PAIR + 1 - side},
        )

    def side_arrival(direction, step, chunk):
        here = k_slot(source(direction, step) * PAIR + 1 - side, chunk)
        return remote(
            here, here, y_send.at[direction, step, chunk], y_recv.at[direction, step, chunk], {"va": va}
        )

    def own_copy(chunk):
        return pltpu.make_async_copy(own_slot(chunk), k_slot(va, chunk), own_sem.at[ratio + 1 + chunk])

    def send_own(chunk):
        for direction in range(2):

            @pl.when(may_send(direction, 0))
            def _():
                line_send(direction, 0, chunk).start()

    side_send(0, 0, early).start()
    for chunk in range(chunks):
        send_own(chunk)
        if chunk != early:
            side_send(0, 0, chunk).start()
    for chunk in range(chunks):
        own_copy(chunk).start()
    side_arrival(0, 0, early).wait_recv()
    send_own(chunks)

    def pass_mirror(part, half):
        mirror_passing(part, half).wait_recv()
        mirror_on(part, half).start()

    each_passing(pass_mirror)

    def line_step(step):
        for chunk in range(chunks + 1):
            for direction in range(2):

                @pl.when(has_arrival(direction, step))
                def _():
                    line_arrival(direction, step, chunk).wait_recv()

                    @pl.when(may_send(direction, step))
                    def _():
                        line_send(direction, step, chunk).start()

                    if chunk < early:
                        side_send(direction, step, chunk).start()

    def spin_send(shift):
        to = lax.rem(outer + shift, outers)
        return remote(
            spin, spin_all.at[vb], s_send.at[0, shift], s_recv.at[0, shift], {"vb": to * PAIR + core}
        )

    def spin_arrival(shift):
        here = spin_all.at[lax.rem(outer + outers - shift, outers) * PAIR + core]
        return remote(here, here, s_send.at[0, shift], s_recv.at[0, shift], {"vb": vb})

    def spin_relay(shift):
        held = spin_all.at[lax.rem(outer + outers - shift, outers) * PAIR + core]
        src = spin if shift == 0 else held
        return remote(
            src, held, s_send.at[1, shift], s_recv.at[1, shift], {"vb": outer * PAIR + 1 - core}
        )

    def relay_arrival(shift):
        here = spin_all.at[lax.rem(outer + outers - shift, outers) * PAIR + 1 - core]
        return remote(here, here, s_send.at[1, shift], s_recv.at[1, shift], {"vb": vb})

    def spin_own():
        return pltpu.make_async_copy(spin, spin_all.at[vb], own_sem.at[ratio])

    def spin_step():
        for part in range(ratio):

            @pl.when(stays(part))
            def _():
                mirror_own(part).wait()

            @pl.when(jnp.logical_not(stays(part)))
            def _():
                for half in range(halves):
                    mirror_arrival(part, half).wait_recv()

            cols = slice(part * row_len, (part + 1) * row_len)
            spin[:, :, :, cols] = (
                2.0 * amp_ref[:, :, :, cols].astype(jnp.float32) - landed[part].astype(jnp.float32)
            ).astype(spin.dtype)
        for shift in range(1, outers):
            spin_send(shift).start()
        spin_relay(0).start()
        spin_own().start()

    spin_after = 1
    for step in range(1, lines):
        line_step(step)
        if step == spin_after:
            spin_step()
    if spin_after == 0:
        spin_step()
    for shift in range(1, outers):
        spin_arrival(shift).wait_recv()
        spin_relay(shift).start()

    for chunk in range(chunks + 1):
        if chunk < chunks:
            own_copy(chunk).wait()
            side_send(0, 0, chunk).wait_send()
            if chunk != early:
                side_arrival(0, 0, chunk).wait_recv()
        for direction in range(2):

            @pl.when(may_send(direction, 0))
            def _():
                line_send(direction, 0, chunk).wait_send()

    for step in range(1, lines):
        for chunk in range(chunks + 1):
            for direction in range(2):

                @pl.when(may_send(direction, step))
                def _():
                    line_send(direction, step, chunk).wait_send()

                if chunk < early:

                    @pl.when(has_arrival(direction, step))
                    def _():
                        side_arrival(direction, step, chunk).wait_recv()
                        side_send(direction, step, chunk).wait_send()

    each_mirror(
        lambda part: None,
        lambda part, half: mirror_straight(part, half).wait_send(),
        lambda part, half: mirror_out(part, half).wait_send(),
    )
    each_passing(lambda part, half: mirror_on(part, half).wait_send())

    spin_own().wait()
    for shift in range(outers):
        relay_arrival(shift).wait_recv()
        spin_relay(shift).wait_send()
    for shift in range(1, outers):
        spin_send(shift).wait_send()


def gather_all(amplitudes, turned, integrals, count_va, count_vb):
    occ_a, occ_b, row_len, col_len = amplitudes.shape
    blocks, rows, cols = integrals.shape
    chunks = blocks * SPLIT
    ratio = count_va // count_vb
    lines = count_va // PAIR
    outers = count_vb // PAIR
    dma = pltpu.SemaphoreType.DMA
    return pl.pallas_call(
        functools.partial(gather_kernel, count_va, count_vb),
        out_shape=(
            jax.ShapeDtypeStruct((blocks, count_va * rows, cols), integrals.dtype),
            jax.ShapeDtypeStruct((count_vb, occ_a, occ_b, row_len, col_len), amplitudes.dtype),
        ),
        in_specs=[pl.BlockSpec(memory_space=pltpu.VMEM)] * 3,
        out_specs=(pl.BlockSpec(memory_space=pl.ANY),) * 2,
        scratch_shapes=[
            pltpu.VMEM(turned.shape, turned.dtype),
            pltpu.VMEM(turned.shape, turned.dtype),
            pltpu.VMEM(amplitudes.shape, amplitudes.dtype),
            dma((2, lines, chunks + 1)),
            dma((2, lines, chunks + 1)),
            dma((2, lines, chunks)),
            dma((2, lines, chunks)),
            dma((2, ratio, occ_a)),
            dma((ratio, occ_a)),
            dma((ratio, occ_a)),
            dma((ratio, occ_a)),
            dma((2, outers)),
            dma((2, outers)),
            dma((ratio + 1 + chunks,)),
        ],
        compiler_params=pltpu.CompilerParams(has_side_effects=True),
    )(amplitudes, turned, integrals)


def cycle_kernel(at, screen, lengths, occ, spin_ref, k_ref, rows_ref, cols_ref, out_ref):
    slot = pl.program_id(0)
    occ_count = spin_ref.shape[1]
    row_len = out_ref.shape[2]

    @pl.when(slot == 0)
    def _():
        out_ref[...] = jnp.zeros_like(out_ref)

    @pl.when(slot < lengths[at[0]])
    def _():
        for j in range(occ_count):
            right = jnp.concatenate([k_ref[k * occ_count + j] for k in range(occ_count)], axis=0)
            for i in range(occ_count):
                left = jnp.concatenate([spin_ref[0, i, k] for k in range(occ_count)], axis=1)
                out_ref[i, j] += jnp.dot(left, right, preferred_element_type=jnp.float32)

    @pl.when(slot == pl.num_programs(0) - 1)
    def _():
        vir_rows = jnp.broadcast_to(rows_ref[0], (TILE, row_len)).T[:, :1]
        for i in range(occ_count):
            for j in range(occ_count):
                bottom = (occ[i] + occ[j] - vir_rows) - cols_ref[0]
                out_ref[i, j] = out_ref[i, j] / bottom


def local(amplitudes, integrals, occ_energy, vir_energy, screen, lengths):
    count_va = lax.axis_size("va")
    count_vb = lax.axis_size("vb")
    occ_a, occ_b, row_len, col_len = amplitudes.shape
    ratio = count_va // count_vb
    cols = integrals.shape[2]
    turned = jnp.transpose(
        amplitudes.reshape(occ_a, occ_b, row_len, ratio, row_len), (3, 0, 1, 4, 2)
    )
    whole_k, spin_all = gather_all(amplitudes, turned, integrals, count_va, count_vb)
    slots = screen.shape[1]
    per_shard = col_len // TILE
    at = jnp.stack([lax.axis_index("va"), lax.axis_index("vb")]).astype(jnp.int32)

    def tile_of(m, at, screen, lengths):
        return jnp.maximum(screen[at[0], jnp.minimum(m, lengths[at[0]] - 1)], 0)

    def spin_at(m, at, screen, lengths, occ):
        tile = tile_of(m, at, screen, lengths)
        return (tile // per_shard, 0, 0, 0, tile % per_shard)

    return pl.pallas_call(
        cycle_kernel,
        out_shape=jax.ShapeDtypeStruct((occ_a, occ_b, row_len, cols), jnp.float32),
        grid_spec=pltpu.PrefetchScalarGridSpec(
            num_scalar_prefetch=4,
            grid=(slots,),
            in_specs=[
                pl.BlockSpec((1, occ_a, occ_b, row_len, TILE), spin_at),
                pl.BlockSpec(
                    (integrals.shape[0], TILE, cols),
                    lambda m, at, screen, lengths, occ: (0, tile_of(m, at, screen, lengths), 0),
                ),
                pl.BlockSpec((1, 1, row_len), lambda m, at, screen, lengths, occ: (at[0], 0, 0)),
                pl.BlockSpec((1, 1, cols), lambda m, at, screen, lengths, occ: (at[1], 0, 0)),
            ],
            out_specs=pl.BlockSpec(
                (occ_a, occ_b, row_len, cols), lambda m, at, screen, lengths, occ: (0, 0, 0, 0)
            ),
        ),
    )(
        at, screen, lengths, occ_energy, spin_all, whole_k,
        vir_energy.reshape(count_va, 1, row_len), vir_energy.reshape(count_vb, 1, cols),
    )


def solution(mesh):
    return jax.shard_map(
        local,
        mesh=mesh,
        in_specs=(P(None, None, "va", "vb"), P(None, "va", "vb"), P(), P(), P(), P()),
        out_specs=P(None, None, "va", "vb"),
        check_vma=False,
    )
```

time: 146 us -> 120 us (0.82)
  the two profiles are of different devices: /device:TPU:18 before, /device:TPU:0 now
where the time goes in v2:
time: 120 us; the launch traced here: 119 us
  Pallas kernels  116 us (97%)
  local copies, waits for them, and re-layouts  2.52 us (2%)
    pallas_call x1, Pallas kernels, gather_all(): pl.pallas_call(functools.partial(gather_kernel, count_va, count_vb), out_...  110 us
    pallas_call x1, Pallas kernels, local(): pl.pallas_call(cycle_kernel, out_shape=jax.ShapeDtypeStruct((occ_a, occ_b...  5.5 us

profile of v2, /device:TPU:0, one launch (start us, length us, event | category | flops | bytes accessed | tf_op | source)
XLA Modules:
  0.0 118.8 jit_solution(17797735321323977601)
XLA Ops:
  0.0 0.7 pad_add_fusion.at
  0.7 1.5 %copy.7 = bf16[2,2,256,512]{2,3,1,0:T(8,128)(2,1)S(1)} copy(bf16[2,2,256,512]{3,2,1,0:T(8,128)(2,1)} %amp_ref.1) | data formatting | bytes 2097152 | tf_op args[0]
  2.1 1.0 copy.10
  3.2 110.1 %shard_map.64 = (bf16[4,2048,512]{2,1,0:T(8,128)(2,1)}, bf16[4,2,2,256,512]{4,3,2,1,0:T(8,128)(2,1)}) custom-call(bf16[2,2,256,512]{3,2,1,0:T(8,128)(2,1)} %amp_ref.1, bf16[2,2,2,256,256]{4,3,2,1,0:T(8,128)(2,1)} %bitcast.8, bf16[4,256,512]{2,1,0:T(8,128)(2,1)} %int_ref.1), custom_call_target="tpu_custom_call" | custom-call | tf_op jit(solution)/shard_map/pallas_call | solution.py:316
  113.3 5.5 %shard_map.65 = f32[2,2,256,512]{3,2,1,0:T(8,128)} custom-call(s32[2]{0:T(128)} %pad_add_fusion.at, s32[8,8]{1,0:T(8,128)} %screen.1, s32[8]{0:T(128)} %lengths.1, f32[2]{0:T(128)} %occ.1, bf16[4,2,2,256,512]{4,3,2,1,0:T(8,128)(2,1)} %get-tuple-element.7.spin_ref, bf16[4,2048,512]{2,1,0:T(8,128)(2,1)} %get-tuple-element.8.k_ref, f32[8,1,256]{2,1,0:T(1,128)} %bitcast.10, ...), custom_call_target="tpu_custom_call" | custom-call | tf_op jit(solution)/shard_map/pallas_call | solution.py:391

commit v3 on v2

--- a/solution.py
+++ b/solution.py
@@ -10,13 +10,19 @@
 TILE = 128
 PAIR = 2
 SPLIT = 2
+GROUP = 2
 MESH = pl.DeviceIdType.MESH
 
 
 def gather_kernel(
-    count_va, count_vb, amp_ref, turned_ref, int_ref, whole_k, spin_all,
-    landed, passing, spin, z_send, z_recv, y_send, y_recv, m_send, m_recv, x_send, x_recv, s_send, s_recv, own_sem,
+    count_va, count_vb, flip, amp_ref, *refs
 ):
+    refs = list(refs)
+    turned_ref = None if flip else refs.pop(0)
+    (
+        int_ref, whole_k, spin_all,
+        landed, passing, spin, z_send, z_recv, y_send, y_recv, m_send, m_recv, x_send, x_recv, s_send, s_recv, own_sem,
+    ) = refs
     va = lax.axis_index("va")
     vb = lax.axis_index("vb")
     ratio = count_va // count_vb
@@ -49,19 +55,29 @@
     def by_relay(half):
         return outers > 1 and half % 2 == 1
 
+    def piece(part):
+        if flip:
+            return amp_ref.at[:, :, :, pl.ds(part * row_len, row_len)]
+        return turned_ref.at[part]
+
+    def half_piece(part, half):
+        if flip:
+            return amp_ref.at[half, :, :, pl.ds(part * row_len, row_len)]
+        return turned_ref.at[part, half]
+
     def mirror_own(part):
-        return pltpu.make_async_copy(turned_ref.at[part], landed.at[part], own_sem.at[part])
+        return pltpu.make_async_copy(piece(part), landed.at[part], own_sem.at[part])
 
     def mirror_straight(part, half):
         return remote(
-            turned_ref.at[part, half], landed.at[va % ratio, half],
+            half_piece(part, half), landed.at[va % ratio, half],
             m_send.at[0, part, half], m_recv.at[va % ratio, half],
             {"va": vb * ratio + part, "vb": va // ratio},
         )
 
     def mirror_out(part, half):
         return remote(
-            turned_ref.at[part, half], passing.at[part, half],
+            half_piece(part, half), passing.at[part, half],
             x_send.at[part, half], x_recv.at[part, half], {"vb": next_vb},
         )
 
@@ -244,9 +260,12 @@
                     mirror_arrival(part, half).wait_recv()
 
             cols = slice(part * row_len, (part + 1) * row_len)
-            spin[:, :, :, cols] = (
-                2.0 * amp_ref[:, :, :, cols].astype(jnp.float32) - landed[part].astype(jnp.float32)
-            ).astype(spin.dtype)
+            for i in range(halves):
+                for k in range(amp_ref.shape[1]):
+                    mirror = landed[part, i, k].astype(jnp.float32)
+                    spin[i, k, :, cols] = (
+                        2.0 * amp_ref[i, k, :, cols].astype(jnp.float32) - (mirror.T if flip else mirror)
+                    ).astype(spin.dtype)
         for shift in range(1, outers):
             spin_send(shift).start()
         spin_relay(0).start()
@@ -305,25 +324,31 @@
         spin_send(shift).wait_send()
 
 
-def gather_all(amplitudes, turned, integrals, count_va, count_vb):
+def gather_all(amplitudes, integrals, count_va, count_vb):
     occ_a, occ_b, row_len, col_len = amplitudes.shape
     blocks, rows, cols = integrals.shape
     chunks = blocks * SPLIT
     ratio = count_va // count_vb
     lines = count_va // PAIR
     outers = count_vb // PAIR
+    flip = row_len % TILE == 0
+    operands = (amplitudes, integrals)
+    if not flip:
+        turned = amplitudes.reshape(occ_a, occ_b, row_len, ratio, row_len)
+        operands = (amplitudes, jnp.transpose(turned, (3, 0, 1, 4, 2)), integrals)
+    mirror_shape = (ratio, occ_a, occ_b, row_len, row_len)
     dma = pltpu.SemaphoreType.DMA
     return pl.pallas_call(
-        functools.partial(gather_kernel, count_va, count_vb),
+        functools.partial(gather_kernel, count_va, count_vb, flip),
         out_shape=(
             jax.ShapeDtypeStruct((blocks, count_va * rows, cols), integrals.dtype),
             jax.ShapeDtypeStruct((count_vb, occ_a, occ_b, row_len, col_len), amplitudes.dtype),
         ),
-        in_specs=[pl.BlockSpec(memory_space=pltpu.VMEM)] * 3,
+        in_specs=[pl.BlockSpec(memory_space=pltpu.VMEM)] * len(operands),
         out_specs=(pl.BlockSpec(memory_space=pl.ANY),) * 2,
         scratch_shapes=[
-            pltpu.VMEM(turned.shape, turned.dtype),
-            pltpu.VMEM(turned.shape, turned.dtype),
+            pltpu.VMEM(mirror_shape, amplitudes.dtype),
+            pltpu.VMEM(mirror_shape, amplitudes.dtype),
             pltpu.VMEM(amplitudes.shape, amplitudes.dtype),
             dma((2, lines, chunks + 1)),
             dma((2, lines, chunks + 1)),
@@ -338,27 +363,35 @@
             dma((ratio + 1 + chunks,)),
         ],
         compiler_params=pltpu.CompilerParams(has_side_effects=True),
-    )(amplitudes, turned, integrals)
-
-
-def cycle_kernel(at, screen, lengths, occ, spin_ref, k_ref, rows_ref, cols_ref, out_ref):
-    slot = pl.program_id(0)
-    occ_count = spin_ref.shape[1]
+    )(*operands)
+
+
+def cycle_kernel(at, screen, lengths, occ, *refs):
+    spin_refs, k_refs = refs[:GROUP], refs[GROUP : 2 * GROUP]
+    rows_ref, cols_ref, out_ref = refs[2 * GROUP :]
+    slot = pl.program_id(0) * GROUP
+    occ_count = out_ref.shape[0]
+    count = lengths[at[0]]
     row_len = out_ref.shape[2]
 
     @pl.when(slot == 0)
     def _():
         out_ref[...] = jnp.zeros_like(out_ref)
 
-    @pl.when(slot < lengths[at[0]])
+    @pl.when(slot < count)
     def _():
+        pairs = [(m, k) for m in range(GROUP) for k in range(occ_count)]
+        live = [(slot + m < count).astype(spin_refs[0].dtype) for m in range(GROUP)]
+        lefts = [
+            jnp.concatenate([spin_refs[m][0, i, k] * live[m] for m, k in pairs], axis=1)
+            for i in range(occ_count)
+        ]
         for j in range(occ_count):
-            right = jnp.concatenate([k_ref[k * occ_count + j] for k in range(occ_count)], axis=0)
+            right = jnp.concatenate([k_refs[m][k * occ_count + j] for m, k in pairs], axis=0)
             for i in range(occ_count):
-                left = jnp.concatenate([spin_ref[0, i, k] for k in range(occ_count)], axis=1)
-                out_ref[i, j] += jnp.dot(left, right, preferred_element_type=jnp.float32)
-
-    @pl.when(slot == pl.num_programs(0) - 1)
+                out_ref[i, j] += jnp.dot(lefts[i], right, preferred_element_type=jnp.float32)
+
+    @pl.when(pl.program_id(0) == pl.num_programs(0) - 1)
     def _():
         vir_rows = jnp.broadcast_to(rows_ref[0], (TILE, row_len)).T[:, :1]
         for i in range(occ_count):
@@ -371,12 +404,8 @@
     count_va = lax.axis_size("va")
     count_vb = lax.axis_size("vb")
     occ_a, occ_b, row_len, col_len = amplitudes.shape
-    ratio = count_va // count_vb
     cols = integrals.shape[2]
-    turned = jnp.transpose(
-        amplitudes.reshape(occ_a, occ_b, row_len, ratio, row_len), (3, 0, 1, 4, 2)
-    )
-    whole_k, spin_all = gather_all(amplitudes, turned, integrals, count_va, count_vb)
+    whole_k, spin_all = gather_all(amplitudes, integrals, count_va, count_vb)
     slots = screen.shape[1]
     per_shard = col_len // TILE
     at = jnp.stack([lax.axis_index("va"), lax.axis_index("vb")]).astype(jnp.int32)
@@ -384,21 +413,27 @@
     def tile_of(m, at, screen, lengths):
         return jnp.maximum(screen[at[0], jnp.minimum(m, lengths[at[0]] - 1)], 0)
 
-    def spin_at(m, at, screen, lengths, occ):
-        tile = tile_of(m, at, screen, lengths)
+    def spin_at(place, m, at, screen, lengths, occ):
+        tile = tile_of(m * GROUP + place, at, screen, lengths)
         return (tile // per_shard, 0, 0, 0, tile % per_shard)
+
+    def k_at(place, m, at, screen, lengths, occ):
+        return (0, tile_of(m * GROUP + place, at, screen, lengths), 0)
 
     return pl.pallas_call(
         cycle_kernel,
         out_shape=jax.ShapeDtypeStruct((occ_a, occ_b, row_len, cols), jnp.float32),
         grid_spec=pltpu.PrefetchScalarGridSpec(
             num_scalar_prefetch=4,
-            grid=(slots,),
+            grid=(pl.cdiv(slots, GROUP),),
             in_specs=[
-                pl.BlockSpec((1, occ_a, occ_b, row_len, TILE), spin_at),
-                pl.BlockSpec(
-                    (integrals.shape[0], TILE, cols),
-                    lambda m, at, screen, lengths, occ: (0, tile_of(m, at, screen, lengths), 0),
+                *(
+                    pl.BlockSpec((1, occ_a, occ_b, row_len, TILE), functools.partial(spin_at, place))
+                    for place in range(GROUP)
+                ),
+                *(
+                    pl.BlockSpec((integrals.shape[0], TILE, cols), functools.partial(k_at, place))
+                    for place in range(GROUP)
                 ),
                 pl.BlockSpec((1, 1, row_len), lambda m, at, screen, lengths, occ: (at[0], 0, 0)),
                 pl.BlockSpec((1, 1, cols), lambda m, at, screen, lengths, occ: (at[1], 0, 0)),
@@ -408,7 +443,7 @@
             ),
         ),
     )(
-        at, screen, lengths, occ_energy, spin_all, whole_k,
+        at, screen, lengths, occ_energy, *[spin_all] * GROUP, *[whole_k] * GROUP,
         vir_energy.reshape(count_va, 1, row_len), vir_energy.reshape(count_vb, 1, cols),
     )
 

time: 120 us -> 118 us (0.983)
  local copies, waits for them, and re-layouts: 2.52 us -> 0 us
    unnamed x1 -> x0, local copies, waits for them, and re-layouts: 1.47 us -> none
where the time goes in v3:
time: 118 us; the launch traced here: 117 us
  Pallas kernels  116 us (98%)
    pallas_call x1, Pallas kernels, gather_all(): pl.pallas_call(functools.partial(gather_kernel, count_va, count_vb, flip)...  110 us
    pallas_call x1, Pallas kernels, local(): pl.pallas_call(cycle_kernel, out_shape=jax.ShapeDtypeStruct((occ_a, occ_b...  6.28 us

profile of v3, /device:TPU:0, one launch (start us, length us, event | category | flops | bytes accessed | tf_op | source)
XLA Modules:
  0.0 116.7 jit_solution(12392716964629495415)
XLA Ops:
  0.0 0.7 pad_add_fusion.at
  0.7 109.8 %shard_map.64 = (bf16[4,2048,512]{2,1,0:T(8,128)(2,1)}, bf16[4,2,2,256,512]{4,3,2,1,0:T(8,128)(2,1)}) custom-call(bf16[2,2,256,512]{3,2,1,0:T(8,128)(2,1)} %amp_ref.1, bf16[4,256,512]{2,1,0:T(8,128)(2,1)} %refs_0_.1), custom_call_target="tpu_custom_call" | custom-call | tf_op jit(solution)/shard_map/pallas_call | solution.py:341
  110.5 6.3 %shard_map.65 = f32[2,2,256,512]{3,2,1,0:T(8,128)} custom-call(s32[2]{0:T(128)} %pad_add_fusion.at, s32[8,8]{1,0:T(8,128)} %screen.1, s32[8]{0:T(128)} %lengths.1, f32[2]{0:T(128)} %occ.1, bf16[4,2,2,256,512]{4,3,2,1,0:T(8,128)(2,1)} %get-tuple-element.7.refs_0_.refs_1_, bf16[4,2,2,256,512]{4,3,2,1,0:T(8,128)(2,1)} %get-tuple-element.7.refs_0_.refs_1_, ...), custom_call_target="tpu_custom_call" | custom-call | tf_op jit(solution)/shard_map/pallas_call | solution.py:423
